TPU v7x, 32 devices: a whole 2x2x4 slice. The times are simulated.
32 devices in a mesh: leaf: 4 (over z), rows: 8 (over y, x, core).
Axes of the slice: x: 2, y: 2, z: 4, core: 2. Of those that a mesh axis runs over, the one named last changes fastest.
Arguments:
- rhs: float32 [131072, 256], P(('leaf', 'rows')), may hold values from -6 to 6
- u_basis: float32 [4, 131072, 128], P(None, ('leaf', 'rows')), may hold values from -0.5 to 0.5
- v_basis: float32 [4, 131072, 128], P(None, ('leaf', 'rows')), may hold values from -0.06629126 to 0.06629126
- cap_inv: float32 [15, 256, 256], replicated, may hold values from -0.1125 to 1.1125
Outputs:
- solved: float32 [131072, 256], P(('leaf', 'rows'))
All inputs are finite; a program needn't handle non-finite values.
Results may differ from a plain program's by a relative error of at most 0.00012.
Values sent between devices are 32-bit elements; how exact they have to be, the bound alone decides.
A program may use at most 128 MiB of HBM per device.

v0:
```python
import jax
import jax.numpy as jnp
from jax import lax
from jax.experimental import pallas as pl
from jax.experimental.pallas import tpu as pltpu
from jax.sharding import PartitionSpec as P

MESH = pl.DeviceIdType.MESH
CHUNK = 512
F32 = jnp.float32
BF16 = jnp.bfloat16


def split(x):
    high = x.astype(BF16)
    return high, (x - high.astype(F32)).astype(BF16)


def dot(a, b):
    return jnp.dot(a, b, preferred_element_type=F32)


def dot_rows(a, b):
    return lax.dot_general(a, b, (((0,), (0,)), ((), ())), preferred_element_type=F32)


def dot3(a, b):
    ah, al = split(a)
    bh, bl = split(b)
    return dot(ah, bh) + dot(al, bh) + dot(ah, bl)


def make_kernel(levels, rows, rank, width, leaves, lines):
    bits = (leaves * lines).bit_length() - 1
    line_bits = lines.bit_length() - 1
    half = rank // 2
    steps = rows // CHUNK
    tops = [bits - level - 1 for level in range(levels)]
    first = [sum(top + 1 for top in tops[:level]) for level in range(levels)]
    exchanges = sum(top + 1 for top in tops)
    widths = [width + level * rank for level in range(levels)]

    def kernel(rhs_hbm, u_hbm, v_hbm, cap_hbm, out_hbm, *scratch):
        rhs, u, v, cap, high, low, coef = scratch[:7]
        acc = scratch[7 : 7 + levels]
        cur = scratch[7 + levels : 7 + 2 * levels]
        recv = scratch[7 + 2 * levels : 7 + 3 * levels]
        stk = scratch[7 + 3 * levels : 7 + 4 * levels]
        rhs_sem, v0_sem, u_sem, v_sem, cap_sem, out_sem, tx, rx = scratch[7 + 4 * levels :]

        leaf = lax.axis_index("leaf")
        line = lax.axis_index("rows")
        flat = leaf * lines + line
        core = line % 2

        def part(index):
            return pl.ds(pl.multiple_of(index * CHUNK, CHUNK), CHUNK)

        rhs_in, v0_in = [], []
        for step in range(steps):
            at = pl.ds(step * CHUNK, CHUNK)
            rhs_in.append(pltpu.make_async_copy(rhs_hbm.at[at], rhs.at[at], rhs_sem.at[step]))
            v0_in.append(pltpu.make_async_copy(v_hbm.at[0, at], v.at[0, at], v0_sem.at[step]))
            rhs_in[-1].start()
            v0_in[-1].start()
        u_in = [pltpu.make_async_copy(u_hbm.at[k], u.at[k], u_sem.at[k]) for k in range(levels)]
        v_in = {k: pltpu.make_async_copy(v_hbm.at[k], v.at[k], v_sem.at[k]) for k in range(1, levels)}
        sides, cap_in = [], []
        for level in range(levels):
            child = flat // (2 ** tops[level])
            side = child % 2
            sides.append(side)
            cap_in.append(
                pltpu.make_async_copy(
                    cap_hbm.at[2**level - 1 + child // 2, pl.ds(pl.multiple_of(side * rank, rank), rank)],
                    cap.at[level],
                    cap_sem.at[level],
                )
            )
        for level in range(1, levels):
            v_in[level].start()
            u_in[level - 1].start()
        u_in[levels - 1].start()
        for copy in cap_in:
            copy.start()

        def partner(bit):
            if bit < line_bits:
                span = 2**bit
                return {"rows": line + span - 2 * span * ((line // span) % 2)}
            span = 2 ** (bit - line_bits)
            return {"leaf": leaf + span - 2 * span * ((leaf // span) % 2)}

        barrier = pltpu.get_barrier_semaphore()
        for bit in range(bits):
            pl.semaphore_signal(barrier, inc=1, device_id=partner(bit), device_id_type=MESH)
        pl.semaphore_wait(barrier, bits)

        mine = pl.ds(pl.multiple_of(core * half, half), half)
        theirs = pl.ds(pl.multiple_of((1 - core) * half, half), half)
        sent = []
        flying = [None] * levels
        stage = [0] * levels

        def send(src, dst, sem, bit):
            copy = pltpu.make_async_remote_copy(
                src_ref=src,
                dst_ref=dst,
                send_sem=tx.at[sem],
                recv_sem=rx.at[sem],
                device_id=partner(bit),
                device_id_type=MESH,
            )
            copy.start()
            sent.append(copy)
            return copy

        def begin(level):
            flying[level] = [send(acc[level].at[theirs], recv[level].at[0], first[level], 0)]

        def advance(level):
            at, top = stage[level], tops[level]
            if at > top + 1:
                return
            for copy in flying[level]:
                copy.wait_recv()
            stage[level] = at + 1
            if at < top:
                own = acc[level][mine] if at == 0 else cur[level][at - 1]
                cur[level][at] = own + recv[level][at]
                flying[level] = [
                    send(cur[level].at[at], recv[level].at[at + 1], first[level] + at + 1, at + 1)
                ]
            elif at == top:
                side = sides[level]
                base = exchanges + 2 * level
                flying[level] = [
                    send(cur[level].at[top - 1], stk[level].at[side, mine], base, 0),
                    send(recv[level].at[top], stk[level].at[1 - side, mine], base + 1, 0),
                ]
                stk[level][side, mine] = cur[level][top - 1]
                stk[level][1 - side, mine] = recv[level][top]

        for level in range(levels):
            columns = widths[level]
            if level:
                v_in[level].wait()
                u_in[level - 1].wait()

            def body(step, level=level, columns=columns):
                at = part(step)
                if level == 0:
                    high[at, :width], low[at, :width] = split(rhs[at])
                else:
                    new = slice(columns - rank, columns)
                    high[at, new], low[at, new] = split(u[level - 1, at])
                vh, vl = split(v[level, at])
                both = dot_rows(jnp.concatenate([vh, vl], axis=1), high[at, :columns])
                acc[level][...] += both[:rank] + both[rank:] + dot_rows(vh, low[at, :columns])

            acc[level][...] = jnp.zeros_like(acc[level])
            if level == 0:
                for step in range(steps):
                    rhs_in[step].wait()
                    v0_in[step].wait()
                    body(step)
            else:
                pl.loop(0, steps)(body)
            begin(level)
            for earlier in range(level):
                advance(earlier)

        u_in[levels - 1].wait()

        @pl.loop(0, steps)
        def _(step):
            at = part(step)
            new = slice(width + (levels - 1) * rank, width + levels * rank)
            high[at, new], low[at, new] = split(u[levels - 1, at])

        for copy in cap_in:
            copy.wait()
        solved = 0
        while solved < levels:
            for level in range(levels - 1, -1, -1):
                advance(level)
            while solved < levels and stage[solved] > tops[solved] + 1:
                level = solved
                proj = stk[level][:, :, :width].reshape(2 * rank, width)
                if level:
                    cross = stk[level][:, :, width:].reshape(2 * rank, level * rank)
                    proj = proj - dot3(cross, coef[: level * rank])
                coef[level * rank : (level + 1) * rank] = dot3(cap[level], proj)
                solved += 1

        out_copies = []
        ch, cl = split(coef[...])

        @pl.loop(0, steps)
        def _(step):
            at = part(step)
            uh = high[at, width:]
            ul = low[at, width:]
            rhs[at] = rhs[at] - (dot(uh, ch) + dot(uh, cl) + dot(ul, ch))
            pltpu.make_async_copy(rhs.at[at], out_hbm.at[at], out_sem.at[step]).start()

        for step in range(steps):
            at = pl.ds(step * CHUNK, CHUNK)
            pltpu.make_async_copy(rhs.at[at], out_hbm.at[at], out_sem.at[step]).wait()
        for copy in sent:
            copy.wait_send()

    scratch_shapes = [
        pltpu.VMEM((rows, width), F32),
        pltpu.VMEM((levels, rows, rank), F32),
        pltpu.VMEM((levels, rows, rank), F32),
        pltpu.VMEM((levels, rank, 2 * rank), F32),
        pltpu.VMEM((rows, width + levels * rank), BF16),
        pltpu.VMEM((rows, width + levels * rank), BF16),
        pltpu.VMEM((levels * rank, width), F32),
        *[pltpu.VMEM((rank, w), F32) for w in widths],
        *[pltpu.VMEM((top, half, w), F32) for top, w in zip(tops, widths)],
        *[pltpu.VMEM((top + 1, half, w), F32) for top, w in zip(tops, widths)],
        *[pltpu.VMEM((2, rank, w), F32) for w in widths],
        pltpu.SemaphoreType.DMA((steps,)),
        pltpu.SemaphoreType.DMA((steps,)),
        pltpu.SemaphoreType.DMA((levels,)),
        pltpu.SemaphoreType.DMA((levels,)),
        pltpu.SemaphoreType.DMA((levels,)),
        pltpu.SemaphoreType.DMA((steps,)),
        pltpu.SemaphoreType.DMA((exchanges + 2 * levels,)),
        pltpu.SemaphoreType.DMA((exchanges + 2 * levels,)),
    ]
    return kernel, scratch_shapes


def solution(mesh):
    leaves, lines = mesh.shape["leaf"], mesh.shape["rows"]

    def per_device(rhs, u_basis, v_basis, cap_inv):
        levels, rows, rank = u_basis.shape
        width = rhs.shape[1]
        kernel, scratch_shapes = make_kernel(levels, rows, rank, width, leaves, lines)
        return pl.pallas_call(
            kernel,
            out_shape=jax.ShapeDtypeStruct((rows, width), F32),
            in_specs=[pl.BlockSpec(memory_space=pl.ANY)] * 4,
            out_specs=pl.BlockSpec(memory_space=pl.ANY),
            scratch_shapes=scratch_shapes,
            compiler_params=pltpu.CompilerParams(
                collective_id=0, has_side_effects=True, vmem_limit_bytes=60 * 2**20
            ),
        )(rhs, u_basis, v_basis, cap_inv)

    in_specs = (
        P(("leaf", "rows"), None),
        P(None, ("leaf", "rows"), None),
        P(None, ("leaf", "rows"), None),
        P(),
    )
    return jax.shard_map(
        per_device, mesh=mesh, in_specs=in_specs, out_specs=P(("leaf", "rows"), None), check_vma=False
    )
```

profile of v0, /device:TPU:1, one launch (start us, length us, event | category | flops | bytes accessed | tf_op | source)
XLA Modules:
  0.0 43.1 jit_solution(9861245825892856650)
XLA Ops:
  0.0 38.6 %shard_map.46 = f32[4096,256]{1,0:T(8,128)} custom-call(f32[4096,256]{1,0:T(8,128)} %rhs_hbm.1, f32[4,4096,128]{2,1,0:T(8,128)} %u_hbm.1, f32[4,4096,128]{2,1,0:T(8,128)} %v_hbm.1, f32[15,256,256]{2,1,0:T(8,128)} %cap_hbm.1), custom_call_target="tpu_custom_call" | custom-call | tf_op jit(solution)/shard_map/pallas_call | solution.py:244
  38.7 4.5 %copy.6 = f32[4096,256]{1,0:T(8,128)} copy(f32[4096,256]{1,0:T(8,128)} %shard_map.46) | data formatting | bytes 8388608
where the time goes:
time: 43.3 us; the launch traced here: 43.1 us
  Pallas kernels  38.6 us (89%)
  local copies, waits for them, and re-layouts  4.47 us (10%)
    pallas_call x1, Pallas kernels, per_device(): pl.pallas_call(kernel, out_shape=jax.ShapeDtypeStruct((rows, width), F32)...  38.6 us
    unnamed x1, local copies, waits for them, and re-layouts  4.47 us

commit v1 on v0

--- a/solution.py
+++ b/solution.py
@@ -7,6 +7,7 @@
 
 MESH = pl.DeviceIdType.MESH
 CHUNK = 512
+LIMIT = 45 * 2**20
 F32 = jnp.float32
 BF16 = jnp.bfloat16
 
@@ -40,13 +41,13 @@
     exchanges = sum(top + 1 for top in tops)
     widths = [width + level * rank for level in range(levels)]
 
-    def kernel(rhs_hbm, u_hbm, v_hbm, cap_hbm, out_hbm, *scratch):
-        rhs, u, v, cap, high, low, coef = scratch[:7]
-        acc = scratch[7 : 7 + levels]
-        cur = scratch[7 + levels : 7 + 2 * levels]
-        recv = scratch[7 + 2 * levels : 7 + 3 * levels]
-        stk = scratch[7 + 3 * levels : 7 + 4 * levels]
-        rhs_sem, v0_sem, u_sem, v_sem, cap_sem, out_sem, tx, rx = scratch[7 + 4 * levels :]
+    def kernel(rhs_hbm, u_hbm, v_hbm, cap_hbm, rhs, high, low, coef, *scratch):
+        u, v, cap = scratch[:3]
+        acc = scratch[3 : 3 + levels]
+        cur = scratch[3 + levels : 3 + 2 * levels]
+        recv = scratch[3 + 2 * levels : 3 + 3 * levels]
+        stk = scratch[3 + 3 * levels : 3 + 4 * levels]
+        rhs_sem, v0_sem, u_sem, v_sem, cap_sem, tx, rx = scratch[3 + 4 * levels :]
 
         leaf = lax.axis_index("leaf")
         line = lax.axis_index("rows")
@@ -120,7 +121,7 @@
 
         def advance(level):
             at, top = stage[level], tops[level]
-            if at > top + 1:
+            if at > top:
                 return
             for copy in flying[level]:
                 copy.wait_recv()
@@ -131,15 +132,27 @@
                 flying[level] = [
                     send(cur[level].at[at], recv[level].at[at + 1], first[level] + at + 1, at + 1)
                 ]
-            elif at == top:
-                side = sides[level]
-                base = exchanges + 2 * level
-                flying[level] = [
-                    send(cur[level].at[top - 1], stk[level].at[side, mine], base, 0),
-                    send(recv[level].at[top], stk[level].at[1 - side, mine], base + 1, 0),
-                ]
-                stk[level][side, mine] = cur[level][top - 1]
-                stk[level][1 - side, mine] = recv[level][top]
+
+        def gather(level):
+            while stage[level] <= tops[level]:
+                advance(level)
+            top, side = tops[level], sides[level]
+            pair = jnp.concatenate([cur[level][top - 1], recv[level][top]], axis=0)
+            proj = pair[:, :width]
+            if level:
+                proj = proj - dot3(pair[:, width:], coef[: level * rank])
+            stk[level][side, mine] = proj[:half]
+            stk[level][1 - side, mine] = proj[half:]
+            base = exchanges + 2 * level
+            flying[level] = [
+                send(stk[level].at[k, mine], stk[level].at[k, mine], base + k, 0) for k in range(2)
+            ]
+
+        def finish(level):
+            for copy in flying[level]:
+                copy.wait_recv()
+            stacked = stk[level][...].reshape(2 * rank, width)
+            coef[level * rank : (level + 1) * rank] = dot3(cap[level], stacked)
 
         for level in range(levels):
             columns = widths[level]
@@ -164,12 +177,18 @@
                     rhs_in[step].wait()
                     v0_in[step].wait()
                     body(step)
+            elif level < levels - 1:
+                pl.loop(0, steps)(body)
             else:
-                pl.loop(0, steps)(body)
+                pl.loop(0, steps // 2)(body)
+                for earlier in range(level):
+                    advance(earlier)
+                pl.loop(steps // 2, steps)(body)
             begin(level)
             for earlier in range(level):
                 advance(earlier)
 
+        advance(levels - 1)
         u_in[levels - 1].wait()
 
         @pl.loop(0, steps)
@@ -180,58 +199,71 @@
 
         for copy in cap_in:
             copy.wait()
-        solved = 0
-        while solved < levels:
-            for level in range(levels - 1, -1, -1):
-                advance(level)
-            while solved < levels and stage[solved] > tops[solved] + 1:
-                level = solved
-                proj = stk[level][:, :, :width].reshape(2 * rank, width)
-                if level:
-                    cross = stk[level][:, :, width:].reshape(2 * rank, level * rank)
-                    proj = proj - dot3(cross, coef[: level * rank])
-                coef[level * rank : (level + 1) * rank] = dot3(cap[level], proj)
-                solved += 1
-
-        out_copies = []
-        ch, cl = split(coef[...])
-
-        @pl.loop(0, steps)
-        def _(step):
-            at = part(step)
-            uh = high[at, width:]
-            ul = low[at, width:]
-            rhs[at] = rhs[at] - (dot(uh, ch) + dot(uh, cl) + dot(ul, ch))
-            pltpu.make_async_copy(rhs.at[at], out_hbm.at[at], out_sem.at[step]).start()
-
-        for step in range(steps):
-            at = pl.ds(step * CHUNK, CHUNK)
-            pltpu.make_async_copy(rhs.at[at], out_hbm.at[at], out_sem.at[step]).wait()
+
+        def subtract(start, stop):
+            ch, cl = split(coef[: early * rank])
+            used = slice(width, width + early * rank)
+
+            @pl.loop(start, stop)
+            def _(step):
+                at = part(step)
+                uh, ul = high[at, used], low[at, used]
+                rhs[at] = rhs[at] - (dot(uh, ch) + dot(uh, cl) + dot(ul, ch))
+
+        early = levels // 2
+        for level in range(levels):
+            gather(level)
+            if level == early:
+                subtract(0, steps // 2)
+            if level == levels - 1:
+                subtract(steps // 2, steps)
+            finish(level)
+
         for copy in sent:
             copy.wait_send()
 
+    outs = [
+        pltpu.VMEM((rows, width), F32),
+        pltpu.VMEM((rows, width + levels * rank), BF16),
+        pltpu.VMEM((rows, width + levels * rank), BF16),
+        pltpu.VMEM((levels * rank, width), F32),
+    ]
     scratch_shapes = [
-        pltpu.VMEM((rows, width), F32),
         pltpu.VMEM((levels, rows, rank), F32),
         pltpu.VMEM((levels, rows, rank), F32),
         pltpu.VMEM((levels, rank, 2 * rank), F32),
-        pltpu.VMEM((rows, width + levels * rank), BF16),
-        pltpu.VMEM((rows, width + levels * rank), BF16),
-        pltpu.VMEM((levels * rank, width), F32),
         *[pltpu.VMEM((rank, w), F32) for w in widths],
         *[pltpu.VMEM((top, half, w), F32) for top, w in zip(tops, widths)],
         *[pltpu.VMEM((top + 1, half, w), F32) for top, w in zip(tops, widths)],
-        *[pltpu.VMEM((2, rank, w), F32) for w in widths],
+        *[pltpu.VMEM((2, rank, width), F32) for _ in widths],
         pltpu.SemaphoreType.DMA((steps,)),
         pltpu.SemaphoreType.DMA((steps,)),
         pltpu.SemaphoreType.DMA((levels,)),
         pltpu.SemaphoreType.DMA((levels,)),
         pltpu.SemaphoreType.DMA((levels,)),
-        pltpu.SemaphoreType.DMA((steps,)),
         pltpu.SemaphoreType.DMA((exchanges + 2 * levels,)),
         pltpu.SemaphoreType.DMA((exchanges + 2 * levels,)),
     ]
-    return kernel, scratch_shapes
+    return kernel, outs, scratch_shapes
+
+
+def apply(rhs, high, low, coef, out_hbm, out, out_sem):
+    rows, width = rhs.shape
+    steps = rows // CHUNK
+    early = coef.shape[0] // 2
+    ch, cl = split(coef[early:])
+
+    @pl.loop(0, steps)
+    def _(step):
+        at = pl.ds(pl.multiple_of(step * CHUNK, CHUNK), CHUNK)
+        uh = high[at, width + early :]
+        ul = low[at, width + early :]
+        out[at] = rhs[at] - (dot(uh, ch) + dot(uh, cl) + dot(ul, ch))
+        pltpu.make_async_copy(out.at[at], out_hbm.at[at], out_sem.at[step]).start()
+
+    for step in range(steps):
+        at = pl.ds(step * CHUNK, CHUNK)
+        pltpu.make_async_copy(out.at[at], out_hbm.at[at], out_sem.at[step]).wait()
 
 
 def solution(mesh):
@@ -240,17 +272,26 @@
     def per_device(rhs, u_basis, v_basis, cap_inv):
         levels, rows, rank = u_basis.shape
         width = rhs.shape[1]
-        kernel, scratch_shapes = make_kernel(levels, rows, rank, width, leaves, lines)
-        return pl.pallas_call(
+        kernel, outs, scratch_shapes = make_kernel(levels, rows, rank, width, leaves, lines)
+        whole = pl.BlockSpec(memory_space=pltpu.VMEM)
+        kept = pl.pallas_call(
             kernel,
-            out_shape=jax.ShapeDtypeStruct((rows, width), F32),
+            out_shape=outs,
             in_specs=[pl.BlockSpec(memory_space=pl.ANY)] * 4,
-            out_specs=pl.BlockSpec(memory_space=pl.ANY),
+            out_specs=[whole] * 4,
             scratch_shapes=scratch_shapes,
             compiler_params=pltpu.CompilerParams(
-                collective_id=0, has_side_effects=True, vmem_limit_bytes=60 * 2**20
+                collective_id=0, has_side_effects=True, vmem_limit_bytes=LIMIT
             ),
         )(rhs, u_basis, v_basis, cap_inv)
+        return pl.pallas_call(
+            apply,
+            out_shape=jax.ShapeDtypeStruct((rows, width), F32),
+            in_specs=[whole] * 4,
+            out_specs=pl.BlockSpec(memory_space=pl.ANY),
+            scratch_shapes=[pltpu.VMEM((rows, width), F32), pltpu.SemaphoreType.DMA((rows // CHUNK,))],
+            compiler_params=pltpu.CompilerParams(vmem_limit_bytes=8 * 2**20),
+        )(*kept)
 
     in_specs = (
         P(("leaf", "rows"), None),

time: 43.3 us -> 39.6 us (0.915)
  the two profiles are of different devices: /device:TPU:1 before, /device:TPU:0 now
where the time goes in v1:
time: 39.6 us; the launch traced here: 39.5 us
  Pallas kernels  39.4 us (99%)
    pallas_call x1, Pallas kernels, per_device(): pl.pallas_call(kernel, out_shape=outs, in_specs=[pl.BlockSpec(memory_spac...  35.5 us
    pallas_call x1, Pallas kernels, per_device(): pl.pallas_call(apply, out_shape=jax.ShapeDtypeStruct((rows, width), F32),...  3.92 us

profile of v1, /device:TPU:0, one launch (start us, length us, event | category | flops | bytes accessed | tf_op | source)
XLA Modules:
  0.0 39.5 jit_solution(8966546270132977310)
XLA Ops:
  0.0 35.5 %shard_map.46 = (f32[4096,256]{1,0:T(8,128)S(1)}, bf16[4096,768]{1,0:T(8,128)(2,1)S(1)}, bf16[4096,768]{1,0:T(8,128)(2,1)S(1)}, f32[512,256]{1,0:T(8,128)S(1)}) custom-call(f32[4096,256]{1,0:T(8,128)} %rhs_hbm.1, f32[4,4096,128]{2,1,0:T(8,128)} %u_hbm.1, f32[4,4096,128]{2,1,0:T(8,128)} %v_hbm.1, f32[15,256,256]{2,1,0:T(8,128)} %cap_hbm.1), custom_call_target="tpu_custom_call" | custom-call | tf_op jit(solution)/shard_map/pallas_call | solution.py:277
  35.5 3.9 %shard_map.47 = f32[4096,256]{1,0:T(8,128)} custom-call(f32[4096,256]{1,0:T(8,128)S(1)} %get-tuple-element.9.rhs, bf16[4096,768]{1,0:T(8,128)(2,1)S(1)} %get-tuple-element.10.high, bf16[4096,768]{1,0:T(8,128)(2,1)S(1)} %get-tuple-element.11.low, f32[512,256]{1,0:T(8,128)S(1)} %get-tuple-element.12.coef), custom_call_target="tpu_custom_call" | custom-call | tf_op jit(solution)/shard_map/pallas_call | solution.py:287

commit v2 on v1

--- a/solution.py
+++ b/solution.py
@@ -8,6 +8,7 @@
 MESH = pl.DeviceIdType.MESH
 CHUNK = 512
 LIMIT = 45 * 2**20
+PLAN = {1: ((0,), ()), 2: ((0, 1), (0, 1)), 3: ((2,), (0, 1), (2,), (1, 2))}
 F32 = jnp.float32
 BF16 = jnp.bfloat16
 
@@ -177,25 +178,25 @@
                     rhs_in[step].wait()
                     v0_in[step].wait()
                     body(step)
-            elif level < levels - 1:
-                pl.loop(0, steps)(body)
+                begin(level)
             else:
-                pl.loop(0, steps // 2)(body)
-                for earlier in range(level):
-                    advance(earlier)
-                pl.loop(steps // 2, steps)(body)
-            begin(level)
-            for earlier in range(level):
-                advance(earlier)
-
-        advance(levels - 1)
+                plan = PLAN[level]
+                piece = steps // len(plan)
+                for k, ready in enumerate(plan):
+                    pl.loop(k * piece, (k + 1) * piece)(body)
+                    if k == len(plan) - 1:
+                        begin(level)
+                    for earlier in ready:
+                        advance(earlier)
+
         u_in[levels - 1].wait()
 
-        @pl.loop(0, steps)
-        def _(step):
-            at = part(step)
-            new = slice(width + (levels - 1) * rank, width + levels * rank)
-            high[at, new], low[at, new] = split(u[levels - 1, at])
+        def split_last(start, stop):
+            @pl.loop(start, stop)
+            def _(step):
+                at = part(step)
+                new = slice(width + (levels - 1) * rank, width + levels * rank)
+                high[at, new], low[at, new] = split(u[levels - 1, at])
 
         for copy in cap_in:
             copy.wait()
@@ -211,8 +212,16 @@
                 rhs[at] = rhs[at] - (dot(uh, ch) + dot(uh, cl) + dot(ul, ch))
 
         early = levels // 2
+        quarter = steps // 4
+        gather(0)
+        split_last(0, quarter)
+        advance(levels - 1)
+        split_last(quarter, 3 * quarter)
         for level in range(levels):
-            gather(level)
+            if level:
+                gather(level)
+            if level == 1:
+                split_last(3 * quarter, steps)
             if level == early:
                 subtract(0, steps // 2)
             if level == levels - 1:

time: 39.6 us -> 38 us (0.960)
  Pallas kernels: 39.4 us -> 37.8 us
    pallas_call x1, Pallas kernels: 35.5 us -> 33.9 us  [per_device(): pl.pallas_call(kernel, out_shape=outs, in_specs=[pl.BlockSpec(memory_spac...]
where the time goes in v2:
time: 38 us; the launch traced here: 37.8 us
  Pallas kernels  37.8 us (99%)
    pallas_call x1, Pallas kernels, per_device(): pl.pallas_call(kernel, out_shape=outs, in_specs=[pl.BlockSpec(memory_spac...  33.9 us
    pallas_call x1, Pallas kernels, per_device(): pl.pallas_call(apply, out_shape=jax.ShapeDtypeStruct((rows, width), F32),...  3.92 us

profile of v2, /device:TPU:0, one launch (start us, length us, event | category | flops | bytes accessed | tf_op | source)
XLA Modules:
  0.0 37.8 jit_solution(11618441221519817902)
XLA Ops:
  0.0 33.9 %shard_map.46 = (f32[4096,256]{1,0:T(8,128)S(1)}, bf16[4096,768]{1,0:T(8,128)(2,1)S(1)}, bf16[4096,768]{1,0:T(8,128)(2,1)S(1)}, f32[512,256]{1,0:T(8,128)S(1)}) custom-call(f32[4096,256]{1,0:T(8,128)} %rhs_hbm.1, f32[4,4096,128]{2,1,0:T(8,128)} %u_hbm.1, f32[4,4096,128]{2,1,0:T(8,128)} %v_hbm.1, f32[15,256,256]{2,1,0:T(8,128)} %cap_hbm.1), custom_call_target="tpu_custom_call" | custom-call | tf_op jit(solution)/shard_map/pallas_call | solution.py:286
  33.9 3.9 %shard_map.47 = f32[4096,256]{1,0:T(8,128)} custom-call(f32[4096,256]{1,0:T(8,128)S(1)} %get-tuple-element.9.rhs, bf16[4096,768]{1,0:T(8,128)(2,1)S(1)} %get-tuple-element.10.high, bf16[4096,768]{1,0:T(8,128)(2,1)S(1)} %get-tuple-element.11.low, f32[512,256]{1,0:T(8,128)S(1)} %get-tuple-element.12.coef), custom_call_target="tpu_custom_call" | custom-call | tf_op jit(solution)/shard_map/pallas_call | solution.py:296

commit v3 on v2

--- a/solution.py
+++ b/solution.py
@@ -6,7 +6,7 @@
 from jax.sharding import PartitionSpec as P
 
 MESH = pl.DeviceIdType.MESH
-CHUNK = 512
+CHUNK = 1024
 LIMIT = 45 * 2**20
 PLAN = {1: ((0,), ()), 2: ((0, 1), (0, 1)), 3: ((2,), (0, 1), (2,), (1, 2))}
 F32 = jnp.float32

time: 38 us -> 37 us (0.974)
  Pallas kernels: 37.8 us -> 36.9 us
    pallas_call x1, Pallas kernels: 3.92 us -> 3.37 us  [per_device(): pl.pallas_call(apply, out_shape=jax.ShapeDtypeStruct((rows, width), F32),...]
where the time goes in v3:
time: 37 us; the launch traced here: 36.9 us
  Pallas kernels  36.9 us (100%)
    pallas_call x1, Pallas kernels, per_device(): pl.pallas_call(kernel, out_shape=outs, in_specs=[pl.BlockSpec(memory_spac...  33.5 us
    pallas_call x1, Pallas kernels, per_device(): pl.pallas_call(apply, out_shape=jax.ShapeDtypeStruct((rows, width), F32),...  3.37 us

profile of v3, /device:TPU:0, one launch (start us, length us, event | category | flops | bytes accessed | tf_op | source)
XLA Modules:
  0.0 36.9 jit_solution(4635589755379194517)
XLA Ops:
  0.0 33.5 %shard_map.46 = (f32[4096,256]{1,0:T(8,128)S(1)}, bf16[4096,768]{1,0:T(8,128)(2,1)S(1)}, bf16[4096,768]{1,0:T(8,128)(2,1)S(1)}, f32[512,256]{1,0:T(8,128)S(1)}) custom-call(f32[4096,256]{1,0:T(8,128)} %rhs_hbm.1, f32[4,4096,128]{2,1,0:T(8,128)} %u_hbm.1, f32[4,4096,128]{2,1,0:T(8,128)} %v_hbm.1, f32[15,256,256]{2,1,0:T(8,128)} %cap_hbm.1), custom_call_target="tpu_custom_call" | custom-call | tf_op jit(solution)/shard_map/pallas_call | solution.py:286
  33.5 3.4 %shard_map.47 = f32[4096,256]{1,0:T(8,128)} custom-call(f32[4096,256]{1,0:T(8,128)S(1)} %get-tuple-element.9.rhs, bf16[4096,768]{1,0:T(8,128)(2,1)S(1)} %get-tuple-element.10.high, bf16[4096,768]{1,0:T(8,128)(2,1)S(1)} %get-tuple-element.11.low, f32[512,256]{1,0:T(8,128)S(1)} %get-tuple-element.12.coef), custom_call_target="tpu_custom_call" | custom-call | tf_op jit(solution)/shard_map/pallas_call | solution.py:296
